TPU v7x, 32 devices: a whole 2x2x4 slice. The times are simulated.
32 devices in a mesh: expert: 8 (over z, core), shard: 4 (over y, x).
Axes of the slice: x: 2, y: 2, z: 4, core: 2. Of those that a mesh axis runs over, the one named last changes fastest.
Arguments:
- inputs: float32 [16384, 768], P(('expert', 'shard')), may hold values from -6 to 6
- cotangent: float32 [16384, 768], P(('expert', 'shard')), may hold values from -6 to 6
- norm_one: bfloat16 [768], P('shard'), may hold values from 0.5 to 1.5
- qkv_weight: bfloat16 [768, 2304], P('shard'), may hold values from -0.21875 to 0.21875
- out_weight: bfloat16 [768, 768], P('shard'), may hold values from -3.5 to 3.5
- norm_two: bfloat16 [768], P('shard'), may hold values from 0.5 to 1.5
- shared_gate: bfloat16 [768, 2048], P(None, 'shard'), may hold values from -0.21875 to 0.21875
- shared_up: bfloat16 [768, 2048], P(None, 'shard'), may hold values from -0.21875 to 0.21875
- shared_down: bfloat16 [2048, 768], P('shard'), may hold values from -0.125 to 0.125
- expert_gate: bfloat16 [8, 768, 2048], P('expert'), may hold values from -0.21875 to 0.21875
- expert_up: bfloat16 [8, 768, 2048], P('expert'), may hold values from -0.21875 to 0.21875
- expert_down: bfloat16 [8, 2048, 768], P('expert'), may hold values from -0.125 to 0.125
- gate_weights: float32 [16384, 2], P(('expert', 'shard')), may hold values from 0.25 to 1
- routes: int32 [16384, 2], P(('expert', 'shard')), may hold values from 0 to 7, all different within a row; in each aligned block of 512 rows (0 to 511, 512 to 1023, ...) at most 256 rows name the same one
- prefix: int32 [32], P(('expert', 'shard')), may hold values from 51 to 256
Outputs:
- output: float32 [16384, 768], P(('expert', 'shard'))
- input_grad: float32 [16384, 768], P(('expert', 'shard'))
- norm_one_grad: float32 [768], P('shard')
- qkv_grad: float32 [768, 2304], P('shard')
- out_grad: float32 [768, 768], P('shard')
- norm_two_grad: float32 [768], P('shard')
- shared_gate_grad: float32 [768, 2048], P(None, 'shard')
- shared_up_grad: float32 [768, 2048], P(None, 'shard')
- shared_down_grad: float32 [2048, 768], P('shard')
- expert_gate_grad: float32 [8, 768, 2048], P('expert', None, 'shard')
- expert_up_grad: float32 [8, 768, 2048], P('expert', None, 'shard')
- expert_down_grad: float32 [8, 2048, 768], P('expert', 'shard')
- gate_weights_grad: float32 [16384, 2], P(('expert', 'shard'))
Inputs may be any that keep to these rules, and one draw needn't show every extreme that they name: `routes`: each row names 2 different experts. Among the 512 rows of one device no expert is named more than 256 times, and some device names some expert exactly 256 times. `prefix`: leading tokens of a sequence that all its tokens attend to.
All inputs are finite; a program needn't handle non-finite values.
Results may differ from a plain program's by a relative error of at most 0.02.
Values may be sent and summed in bfloat16 or wider, within the bound.
A program may use at most 256 MiB of HBM per device.

v0:
```python
import jax
import jax.numpy as jnp
from jax import lax
from jax.sharding import PartitionSpec as P

HEADS = 12
HEAD_DIM = 64
TOP = 2
EPS = 1e-06


def rope_tables(length):
    half_dim = HEAD_DIM // 2
    frequency = 10000.0 ** (-jnp.arange(half_dim, dtype=jnp.float32) * 2.0 / HEAD_DIM)
    angles = jnp.arange(length, dtype=jnp.float32)[:, None] * frequency[None, :]
    return (jnp.cos(angles)[:, None, :], jnp.sin(angles)[:, None, :])


def rotate(vectors, cosine_table, sine_table):
    half_dim = vectors.shape[-1] // 2
    first_half = vectors[..., :half_dim]
    second = vectors[..., half_dim:]
    return jnp.concatenate(
        [
            first_half * cosine_table - second * sine_table,
            second * cosine_table + first_half * sine_table,
        ],
        axis=-1,
    )


def gated_unit(pre_gate):
    sigmoid_value = jax.nn.sigmoid(pre_gate)
    activated = pre_gate * sigmoid_value
    derivative = sigmoid_value * (1.0 + pre_gate * (1.0 - sigmoid_value))
    return (activated, derivative)


def norm_back(source, inverse, gain, grad_in):
    scaled = grad_in * gain
    gain_grad = jnp.sum(grad_in * source * inverse, axis=0)
    input_part = inverse * scaled - source * inverse**3 * jnp.mean(
        scaled * source, axis=-1, keepdims=True
    )
    return (gain_grad, input_part)


def matmul(left, right):
    return jnp.dot(left, right, preferred_element_type=jnp.float32)


def on_device(
    inputs,
    cotangent,
    norm_one,
    qkv_weight,
    out_weight,
    norm_two,
    shared_gate,
    shared_up,
    shared_down,
    expert_gate,
    expert_up,
    expert_down,
    gate_weights,
    routes,
    prefix,
):
    length, model_width = inputs.shape
    qkv_full, out_full, gain_one = (
        lax.all_gather(qkv_weight, "shard", axis=0, tiled=True),
        lax.all_gather(out_weight, "shard", axis=0, tiled=True),
        lax.all_gather(norm_one, "shard", axis=0, tiled=True),
    )
    gate_full, up_full, down_full, gain_two = (
        lax.all_gather(shared_gate, "shard", axis=1, tiled=True),
        lax.all_gather(shared_up, "shard", axis=1, tiled=True),
        lax.all_gather(shared_down, "shard", axis=0, tiled=True),
        lax.all_gather(norm_two, "shard", axis=0, tiled=True),
    )
    gain_one = gain_one.astype(jnp.float32)
    gain_two = gain_two.astype(jnp.float32)
    inverse_one = lax.rsqrt(jnp.mean(inputs * inputs, axis=-1, keepdims=True) + EPS)
    normed_one = (inputs * inverse_one * gain_one).astype(jnp.bfloat16)
    projected = matmul(normed_one, qkv_full)
    cosine_table, sine_table = rope_tables(length)
    head_shape = (length, HEADS, HEAD_DIM)
    queries = rotate(
        projected[:, :model_width].reshape(head_shape), cosine_table, sine_table
    ).astype(jnp.bfloat16)
    key_rows = rotate(
        projected[:, model_width : 2 * model_width].reshape(head_shape), cosine_table, sine_table
    ).astype(jnp.bfloat16)
    value_rows = projected[:, 2 * model_width :].reshape(head_shape).astype(jnp.bfloat16)
    score_scale = HEAD_DIM ** (-0.5)
    row_pos = lax.broadcasted_iota(jnp.int32, (length, length), 0)
    col_pos = lax.broadcasted_iota(jnp.int32, (length, length), 1)
    visible = (col_pos < prefix[0]) | (col_pos <= row_pos)

    def masked_scores():
        raw_scores = (
            jnp.einsum("qhd,khd->hqk", queries, key_rows, preferred_element_type=jnp.float32)
            * score_scale
        )
        return jnp.where(visible[None], raw_scores, -1e30)

    scores = masked_scores()
    row_peak = jnp.max(scores, axis=-1, keepdims=True)
    exponent = jnp.exp(scores - row_peak)
    expsum = jnp.sum(exponent, axis=-1, keepdims=True)
    logsum = row_peak + jnp.log(expsum)
    probs_low = (exponent / expsum).astype(jnp.bfloat16)
    attended = (
        jnp.einsum("hqk,khd->qhd", probs_low, value_rows, preferred_element_type=jnp.float32)
        .reshape(length, model_width)
        .astype(jnp.bfloat16)
    )
    resid = inputs + matmul(attended, out_full)
    inverse_two = lax.rsqrt(jnp.mean(resid * resid, axis=-1, keepdims=True) + EPS)
    normed_two = (resid * inverse_two * gain_two).astype(jnp.bfloat16)
    shared_pre = matmul(normed_two, gate_full)
    shared_lift = matmul(normed_two, up_full)
    shared_act, shared_slope = gated_unit(shared_pre)
    shared_hidden = (shared_act * shared_lift).astype(jnp.bfloat16)
    shared_out = matmul(shared_hidden, down_full)
    experts = lax.axis_size("expert") * expert_gate.shape[0]
    capacity = 4 * length // experts
    copies = length * TOP
    flat_route = routes.reshape(copies)
    onehot = (flat_route[:, None] == jnp.arange(experts, dtype=jnp.int32)[None, :]).astype(
        jnp.int32
    )
    slot_index = jnp.sum((jnp.cumsum(onehot, axis=0) - onehot) * onehot, axis=1)
    position = flat_route * capacity + slot_index
    source = (
        jnp.full((experts * capacity,), copies, jnp.int32)
        .at[position]
        .set(jnp.arange(copies, dtype=jnp.int32))
    )
    token_index = jnp.where(source < copies, source // TOP, length)
    copy_index = jnp.where(source < copies, source, copies)

    def place_rows(row_block, index):
        padded = jnp.concatenate([row_block, jnp.zeros((1, model_width), row_block.dtype)], axis=0)
        return padded[index].reshape(experts, capacity, model_width)

    dispatched = place_rows(normed_two, token_index)
    gate_local = expert_gate[0]
    up_local = expert_up[0]
    down_local = expert_down[0]
    received = lax.all_to_all(dispatched, "expert", split_axis=0, concat_axis=0, tiled=True)
    row_count = received.shape[0] * received.shape[1]
    row_block = received.reshape(row_count, model_width)
    pre_gate = matmul(row_block, gate_local)
    pre_up = matmul(row_block, up_local)
    activated, unused_slope = gated_unit(pre_gate)
    hidden = (activated * pre_up).astype(jnp.bfloat16)
    result = matmul(hidden, down_local).astype(jnp.bfloat16).reshape(received.shape)
    returned = lax.all_to_all(result, "expert", split_axis=0, concat_axis=0, tiled=True)
    hidden_shape = (received.shape[0], received.shape[1], pre_gate.shape[1])
    outcome = (returned, received, pre_gate.reshape(hidden_shape), pre_up.reshape(hidden_shape))
    returned, kept_rows, kept_gate, kept_up = outcome
    picked = (
        returned.reshape(experts * capacity, model_width)[position]
        .astype(jnp.float32)
        .reshape(length, TOP, model_width)
    )
    mixture = jnp.sum(gate_weights[:, :, None] * picked, axis=1)
    output = resid + mixture + shared_out
    gate_weights_grad = jnp.sum(cotangent[:, None, :] * picked, axis=2)
    copy_grad = (
        (gate_weights[:, :, None] * cotangent[:, None, :])
        .astype(jnp.bfloat16)
        .reshape(copies, model_width)
    )
    grad_send = place_rows(copy_grad, copy_index)
    grad_recv = lax.all_to_all(grad_send, "expert", split_axis=0, concat_axis=0, tiled=True)
    row_count = kept_rows.shape[0] * kept_rows.shape[1]
    rows_flat = kept_rows.reshape(row_count, model_width)
    pre_gate = kept_gate.reshape(row_count, -1)
    pre_up = kept_up.reshape(row_count, -1)
    grad_flat = grad_recv.reshape(row_count, model_width)
    activated, derivative = gated_unit(pre_gate)
    hidden_grad = matmul(grad_flat, down_local.T)
    gate_pre_grad = (hidden_grad * pre_up * derivative).astype(jnp.bfloat16)
    up_pre_grad = (hidden_grad * activated).astype(jnp.bfloat16)
    row_grad = (
        (matmul(gate_pre_grad, gate_local.T) + matmul(up_pre_grad, up_local.T))
        .astype(jnp.bfloat16)
        .reshape(kept_rows.shape)
    )
    row_returned = lax.all_to_all(row_grad, "expert", split_axis=0, concat_axis=0, tiled=True)
    hidden = (activated * pre_up).astype(jnp.bfloat16)
    gate_term = matmul(rows_flat.T, gate_pre_grad)
    up_term = matmul(rows_flat.T, up_pre_grad)
    down_term = matmul(hidden.T, grad_flat)
    expert_gate_grad, expert_up_grad, expert_down_grad = (
        lax.psum_scatter(
            gate_term[None].astype(jnp.bfloat16), "shard", scatter_dimension=2, tiled=True
        ).astype(jnp.float32),
        lax.psum_scatter(
            up_term[None].astype(jnp.bfloat16), "shard", scatter_dimension=2, tiled=True
        ).astype(jnp.float32),
        lax.psum_scatter(
            down_term[None].astype(jnp.bfloat16), "shard", scatter_dimension=1, tiled=True
        ).astype(jnp.float32),
    )
    copy_back = (
        row_returned.reshape(experts * capacity, model_width)[position]
        .astype(jnp.float32)
        .reshape(length, TOP, model_width)
    )
    out_low = cotangent.astype(jnp.bfloat16)
    shared_down_grad = matmul(shared_hidden.T, out_low)
    shared_hgrad = matmul(out_low, down_full.T)
    shared_pre_grad = (shared_hgrad * shared_lift * shared_slope).astype(jnp.bfloat16)
    shared_lift_grad = (shared_hgrad * shared_act).astype(jnp.bfloat16)
    shared_gate_grad = matmul(normed_two.T, shared_pre_grad)
    shared_up_grad = matmul(normed_two.T, shared_lift_grad)
    normed_two_grad = (
        matmul(shared_pre_grad, gate_full.T)
        + matmul(shared_lift_grad, up_full.T)
        + jnp.sum(copy_back, axis=1)
    )
    gain_two_grad, resid_extra = norm_back(resid, inverse_two, gain_two, normed_two_grad)
    resid_grad = cotangent + resid_extra
    ffn_pieces = (
        lax.psum_scatter(
            shared_gate_grad.astype(jnp.bfloat16), "shard", scatter_dimension=1, tiled=True
        ).astype(jnp.float32),
        lax.psum_scatter(
            shared_up_grad.astype(jnp.bfloat16), "shard", scatter_dimension=1, tiled=True
        ).astype(jnp.float32),
        lax.psum_scatter(
            shared_down_grad.astype(jnp.bfloat16), "shard", scatter_dimension=0, tiled=True
        ).astype(jnp.float32),
        lax.psum_scatter(
            gain_two_grad.astype(jnp.bfloat16), "shard", scatter_dimension=0, tiled=True
        ).astype(jnp.float32),
    )
    attn_low = resid_grad.astype(jnp.bfloat16)
    out_weight_grad = matmul(attended.T, attn_low)
    attended_grad = matmul(attn_low, out_full.T).astype(jnp.bfloat16).reshape(head_shape)
    scores = masked_scores()
    probs_full = jnp.exp(scores - logsum)
    value_grad = jnp.einsum(
        "hqk,qhd->khd",
        probs_full.astype(jnp.bfloat16),
        attended_grad,
        preferred_element_type=jnp.float32,
    )
    probs_grad = jnp.einsum(
        "qhd,khd->hqk", attended_grad, value_rows, preferred_element_type=jnp.float32
    )
    score_grad = (
        probs_full * (probs_grad - jnp.sum(probs_full * probs_grad, axis=-1, keepdims=True))
    ).astype(jnp.bfloat16)
    query_grad = (
        jnp.einsum("hqk,khd->qhd", score_grad, key_rows, preferred_element_type=jnp.float32)
        * score_scale
    )
    key_grad = (
        jnp.einsum("hqk,qhd->khd", score_grad, queries, preferred_element_type=jnp.float32)
        * score_scale
    )
    projected_grad = jnp.concatenate(
        [
            rotate(query_grad, cosine_table, -sine_table).reshape(length, model_width),
            rotate(key_grad, cosine_table, -sine_table).reshape(length, model_width),
            value_grad.reshape(length, model_width),
        ],
        axis=1,
    ).astype(jnp.bfloat16)
    qkv_weight_grad = matmul(normed_one.T, projected_grad)
    normed_one_grad = matmul(projected_grad, qkv_full.T)
    gain_one_grad, input_extra = norm_back(inputs, inverse_one, gain_one, normed_one_grad)
    input_grad = resid_grad + input_extra
    attn_pieces = (
        lax.psum_scatter(
            qkv_weight_grad.astype(jnp.bfloat16), "shard", scatter_dimension=0, tiled=True
        ).astype(jnp.float32),
        lax.psum_scatter(
            out_weight_grad.astype(jnp.bfloat16), "shard", scatter_dimension=0, tiled=True
        ).astype(jnp.float32),
        lax.psum_scatter(
            gain_one_grad.astype(jnp.bfloat16), "shard", scatter_dimension=0, tiled=True
        ).astype(jnp.float32),
    )
    summed = (
        lax.psum(attn_pieces[0].astype(jnp.bfloat16), "expert").astype(jnp.float32),
        lax.psum(attn_pieces[1].astype(jnp.bfloat16), "expert").astype(jnp.float32),
        lax.psum(attn_pieces[2].astype(jnp.bfloat16), "expert").astype(jnp.float32),
        lax.psum(ffn_pieces[0].astype(jnp.bfloat16), "expert").astype(jnp.float32),
        lax.psum(ffn_pieces[1].astype(jnp.bfloat16), "expert").astype(jnp.float32),
        lax.psum(ffn_pieces[2].astype(jnp.bfloat16), "expert").astype(jnp.float32),
        lax.psum(ffn_pieces[3].astype(jnp.bfloat16), "expert").astype(jnp.float32),
    )
    return (
        output,
        input_grad,
        summed[2],
        summed[0],
        summed[1],
        summed[6],
        summed[3],
        summed[4],
        summed[5],
        expert_gate_grad,
        expert_up_grad,
        expert_down_grad,
        gate_weights_grad,
    )


def solution(mesh):
    in_specs = (
        P(("expert", "shard"), None),
        P(("expert", "shard"), None),
        P("shard"),
        P("shard", None),
        P("shard", None),
        P("shard"),
        P(None, "shard"),
        P(None, "shard"),
        P("shard", None),
        P("expert", None, None),
        P("expert", None, None),
        P("expert", None, None),
        P(("expert", "shard"), None),
        P(("expert", "shard"), None),
        P(("expert", "shard")),
    )
    out_specs = (
        P(("expert", "shard"), None),
        P(("expert", "shard"), None),
        P("shard"),
        P("shard", None),
        P("shard", None),
        P("shard"),
        P(None, "shard"),
        P(None, "shard"),
        P("shard", None),
        P("expert", None, "shard"),
        P("expert", None, "shard"),
        P("expert", "shard", None),
        P(("expert", "shard"), None),
    )
    return jax.shard_map(
        on_device, mesh=mesh, in_specs=in_specs, out_specs=out_specs, check_vma=False
    )
```

profile of v0, /device:TPU:0, one launch (start us, length us, event | category | flops | bytes accessed | tf_op | source)
XLA Modules:
  0.0 837.4 jit_solution(5135879969428653697)
XLA Ops:
  11.2 4.1 mul.524
  15.3 5.3 mul.525
  29.8 4.3 scatter_custom_fusion
  34.1 11.7 %gather_fusion.2 = bf16[2048,768]{1,0:T(8,128)(2,1)} fusion(bf16[1025,768]{1,0:T(8,128)(2,1)} %concatenate.29, s32[2048]{0:T(1024)S(1)} %get-tuple-element.63), kind=kCustom, calls=%fused_computation.2 | custom fusion | bytes 6299648 | tf_op jit(solution)/shard_map/gather | solution.py:145
  45.8 6.6 all-to-all-start.2
  54.9 10.7 %all-reduce.9 = (bf16[768]{0:T(1024)(128)(2,1)S(1)}, bf16[768]{0:T(1024)(128)(2,1)}) all-reduce(bf16[768]{0:T(1024)(128)(2,1)S(1)} %dynamic-update-slice, bf16[768]{0:T(1024)(128)(2,1)S(1)} %dynamic-update-slice.1), channel_id=1, replica_groups=mesh['expert'=8,'shard'=4] {'shard'}, use_global_device_ids=true, to_apply=%add.2 | all-reduce | flops 1536 | bytes 6144
  70.2 4.5 fusion.59
  86.4 5.8 fusion.7
  96.9 8.0 fusion.1
  105.8 5.9 fusion.28
  116.9 18.3 %all-gather.10.cloned.1.call-done = bf16[768,2048]{1,0:T(8,128)(2,1)} async-done(((bf16[768,512]{1,0:T(8,128)(2,1)}), bf16[768,2048]{1,0:T(8,128)(2,1)}) %all-gather.10.cloned.1.call-update) | async-done | bytes 3145744 | tf_op jit(solution)/shard_map/all_gather | solution.py:76
  135.2 5.9 fusion.62
  141.1 39.6 %all-gather.12.cloned.1.call-done = bf16[768,2048]{1,0:T(8,128)(2,1)} async-done(((bf16[768,512]{1,0:T(8,128)(2,1)}), bf16[768,2048]{1,0:T(8,128)(2,1)}) %all-gather.12.cloned.1.call-update) | async-done | bytes 3145744 | tf_op jit(solution)/shard_map/all_gather | solution.py:77
  180.7 5.9 fusion.63
  186.7 39.8 %all-gather.14.cloned.1.call-done = bf16[2048,768]{1,0:T(8,128)(2,1)} async-done(((bf16[512,768]{1,0:T(8,128)(2,1)}), bf16[2048,768]{1,0:T(8,128)(2,1)}) %all-gather.14.cloned.1.call-update) | async-done | bytes 3145744 | tf_op jit(solution)/shard_map/all_gather | solution.py:78
  226.4 10.0 %multiply_convert_fusion.4 = (bf16[512,2048]{1,0:T(8,128)(2,1)}, bf16[512,2048]{1,0:T(8,128)(2,1)S(1)}, bf16[512,2048]{1,0:T(8,128)(2,1)}) fusion(f32[512,2048]{1,0:T(8,128)} %fusion.62, f32[512,2048]{1,0:T(8,128)} %fusion.63, bf16[2048,768]{1,0:T(8,128)(2,1)} %all-gather.14.cloned.1.call-done, f32[512,768]{1,0:T(8,128)} %param.16), kind=kOutput, calls=%fused_computation.24 | convolution fusion | flops 1626734592 | bytes 19398656 | tf_op jit(solution)/shard_map/dot_general | solution.py:49
  243.3 11.4 %gather_fusion = bf16[2048,768]{1,0:T(8,128)(2,1)} fusion(bf16[513,768]{1,0:T(8,128)(2,1)} %concatenate.28, s32[2048]{0:T(1024)S(1)} %get-tuple-element.64), kind=kCustom, calls=%fused_computation | custom fusion | bytes 6299648 | tf_op jit(solution)/shard_map/gather | solution.py:145
  254.7 4.6 all-to-all-start
  259.3 5.5 convolution_convert_fusion.5
  264.8 12.8 %fusion.9 = f32[2048,2048]{1,0:T(8,128)} fusion(bf16[2048,768]{1,0:T(8,128)(2,1)} %bitcast.18, bf16[1,2048,768]{2,1,0:T(8,128)(2,1)} %param.26), kind=kOutput, calls=%fused_computation.36 | convolution fusion | flops 6442450944 | bytes 23068672 | tf_op jit(solution)/shard_map/dot_general | solution.py:49
  277.6 53.3 %all-to-all-done = bf16[8,256,768]{2,1,0:T(8,128)(2,1)} async-done(((bf16[8,256,768]{2,1,0:T(8,128)(2,1)}), bf16[8,256,768]{2,1,0:T(8,128)(2,1)}, u32[]{:S(2)}, u32[]{:S(2)}) %all-to-all-start) | async-done | bytes 3145760 | tf_op jit(solution)/shard_map/all_to_all | solution.py:151
  330.9 12.6 %fusion.14 = f32[2048,2048]{1,0:T(8,128)} fusion(bf16[2048,768]{1,0:T(8,128)(2,1)} %bitcast.11, bf16[1,768,2048]{2,1,0:T(8,128)(2,1)} %param.25), kind=kOutput, calls=%fused_computation.41 | convolution fusion | flops 6442450944 | bytes 23068672 | tf_op jit(solution)/shard_map/dot_general | solution.py:49
  343.5 26.2 %multiply_convert_fusion.1 = (bf16[2048,2048]{1,0:T(8,128)(2,1)}, bf16[2048,2048]{1,0:T(8,128)(2,1)}, bf16[2048,2048]{1,0:T(8,128)(2,1)}) fusion(f32[2048,2048]{1,0:T(8,128)} %fusion.9, f32[2048,2048]{1,0:T(8,128)} %fusion.14, bf16[2048,768]{1,0:T(8,128)(2,1)} %bitcast.11, bf16[1,768,2048]{2,1,0:T(8,128)(2,1)S(1)} %copy-done), kind=kOutput, calls=%fused_computation.6 | convolution fusion | flops 6505365504 | bytes 65011712 | tf_op jit(solution)/shard_map/dot_general | solution.py:49
  369.7 10.4 %fusion.12 = f32[2048,768]{1,0:T(8,128)S(1)} fusion(bf16[2048,2048]{1,0:T(8,128)(2,1)} %get-tuple-element.44, bf16[1,768,2048]{2,1,0:T(8,128)(2,1)} %param.25), kind=kOutput, calls=%fused_computation.39 | convolution fusion | flops 6442450944 | bytes 17825792 | tf_op jit(solution)/shard_map/dot_general | solution.py:49
  380.2 8.2 add_convert_fusion
  392.0 5.6 convolution_convert_fusion.4
  398.4 5.5 fusion.64
  403.9 59.5 %all-to-all-done.3 = bf16[8,256,768]{2,1,0:T(8,128)(2,1)S(1)} async-done(((bf16[8,256,768]{2,1,0:T(8,128)(2,1)}), bf16[8,256,768]{2,1,0:T(8,128)(2,1)S(1)}, u32[]{:S(2)}, u32[]{:S(2)}) %all-to-all-start.3) | async-done | bytes 3145760 | tf_op jit(solution)/shard_map/all_to_all | solution.py:192
  463.4 5.6 gather_fusion.3
  469.0 4.9 reshape.294
  473.9 5.7 reduce_sum.116
  479.7 5.2 multiply_reduce_fusion.3
  493.2 11.4 %multiply_reduce_fusion = (f32[12,512]{1,0:T(8,128)S(1)}, f32[12,512,512]{1,2,0:T(8,128)}) fusion(f32[12,512]{1,0:T(8,128)S(1)} %log_add_fusion, f32[12,512,512]{1,2,0:T(8,128)} %get-tuple-element.75, pred[512,512]{0,1:T(8,128)(4,1)S(1)} %copy-done.13, bf16[512,12,64]{0,2,1:T(8,128)(2,1)} %bitcast.126, bf16[512,12,64]{0,2,1:T(8,128)(2,1)S(1)} %bitcast.125), kind=kOutput, calls=%fused_computation.11 | convolution fusion | flops 418375680 | bytes 27049984 | tf_op jit(solution)/shard_map/qhd,khd->hqk/dot_general | solution.py:252
  506.0 10.1 %multiply_convert_fusion.3 = bf16[12,512,512]{1,2,0:T(8,128)(2,1)} fusion(f32[12,512,512]{1,2,0:T(8,128)} %get-tuple-element.80, f32[12,512]{1,0:T(8,128)S(1)} %get-tuple-element.79, f32[12,512]{1,0:T(8,128)S(1)} %log_add_fusion, f32[12,512,512]{1,2,0:T(8,128)S(1)} %bitcast.115, pred[512,512]{0,1:T(8,128)(4,1)S(1)} %copy-done.13), kind=kLoop, calls=%fused_computation.10 | loop fusion | flops 18874368 | bytes 31768576 | tf_op jit(solution)/shard_map/convert_element_type | solution.py:257
  533.1 12.2 %fusion.21 = bf16[1,768,2048]{2,1,0:T(8,128)(2,1)} fusion(bf16[2048,768]{1,0:T(8,128)(2,1)} %bitcast.11, bf16[2048,2048]{1,0:T(8,128)(2,1)} %get-tuple-element.43), kind=kOutput, calls=%fused_computation.51 | convolution fusion | flops 6444023808 | bytes 14680064 | tf_op jit(solution)/shard_map/dot_general | solution.py:49
  545.4 12.2 %fusion.22 = bf16[1,768,2048]{2,1,0:T(8,128)(2,1)} fusion(bf16[2048,768]{1,0:T(8,128)(2,1)} %bitcast.11, bf16[2048,2048]{1,0:T(8,128)(2,1)} %get-tuple-element.44), kind=kOutput, calls=%fused_computation.52 | convolution fusion | flops 6444023808 | bytes 14680064 | tf_op jit(solution)/shard_map/dot_general | solution.py:49
  557.7 11.6 %fusion.20 = bf16[1,2048,768]{2,1,0:T(8,128)(2,1)} fusion(bf16[2048,2048]{1,0:T(8,128)(2,1)} %get-tuple-element.45, bf16[2048,768]{1,0:T(8,128)(2,1)} %bitcast.18), kind=kOutput, calls=%fused_computation.50 | convolution fusion | flops 6444023808 | bytes 14680064 | tf_op jit(solution)/shard_map/dot_general | solution.py:49
  571.2 10.2 %convolution_convert_fusion.3 = bf16[2048,768]{1,0:T(8,128)(2,1)} fusion(bf16[2048,2048]{1,0:T(8,128)(2,1)} %get-tuple-element.45, bf16[1,2048,768]{2,1,0:T(8,128)(2,1)S(1)} %copy-done.58), kind=kOutput, calls=%fused_computation.31 | convolution fusion | flops 6444023808 | bytes 14680064 | tf_op jit(solution)/shard_map/dot_general | solution.py:49
  585.8 70.8 %all-to-all-done.1 = bf16[8,256,768]{2,1,0:T(8,128)(2,1)S(1)} async-done(((bf16[8,256,768]{2,1,0:T(8,128)(2,1)}), bf16[8,256,768]{2,1,0:T(8,128)(2,1)S(1)}, u32[]{:S(2)}, u32[]{:S(2)}) %all-to-all-start.1) | async-done | bytes 3145760 | tf_op jit(solution)/shard_map/all_to_all | solution.py:159
  656.6 5.4 gather_fusion.1
  662.0 5.0 reshape.293
  667.1 5.6 multiply_reduce_fusion.4
  672.7 9.1 %all-reduce.8 = (bf16[768]{0:T(1024)(128)(2,1)S(1)}, bf16[768]{0:T(1024)(128)(2,1)S(1)}) all-reduce(bf16[768]{0:T(1024)(128)(2,1)S(1)} %get-tuple-element.30, bf16[768]{0:T(1024)(128)(2,1)S(1)} %get-tuple-element.28), channel_id=2, replica_groups=mesh['expert'=8,'shard'=4] {'shard'}, use_global_device_ids=true, to_apply=%region_14.15.clone | all-reduce | flops 1536 | bytes 6144
  682.0 13.6 %all-reduce.6 = (bf16[192]{0:T(256)(128)(2,1)S(1)}, bf16[192]{0:T(256)(128)(2,1)S(1)}) all-reduce(bf16[192]{0:T(256)(128)(2,1)S(1)} %dynamic-slice.3, bf16[192]{0:T(256)(128)(2,1)S(1)} %dynamic-slice.5), channel_id=1, replica_groups=mesh['expert'=8,'shard'=4] {'expert'}, use_global_device_ids=true, to_apply=%region_15.16 | all-reduce | flops 384 | bytes 1536 | tf_op jit(solution)/shard_map/psum | solution.py:292
  696.8 9.7 %multiply_reduce_fusion.1 = (f32[512,2]{1,0:T(8,128)}, f32[512,768]{1,0:T(8,128)}) fusion(f32[512,2,768]{2,1,0:T(2,128)} %reshape.293, f32[512,768]{1,0:T(8,128)} %param.16, f32[512,2]{1,0:T(8,128)S(1)} %copy-done.19), kind=kLoop, calls=%fused_computation.47 | loop fusion | flops 2751488 | bytes 6299648 | tf_op jit(solution)/shard_map/reduce_sum | solution.py:170
  712.2 4.6 add_add_fusion.1
  721.8 11.9 %reduce-scatter.23.cloned.1.call-done = bf16[1,512,768]{2,1,0:T(8,128)(2,1)} async-done(((bf16[1,2048,768]{2,1,0:T(8,128)(2,1)}), bf16[1,512,768]{2,1,0:T(8,128)(2,1)}) %reduce-scatter.23.cloned.1.call-update) | async-done | bytes 786448 | tf_op jit(solution)/shard_map/reduce_scatter | solution.py:204
  736.1 85.9 %all-reduce.12.cloned.1.call-done = (bf16[192,2304]{1,0:T(8,128)(2,1)}, bf16[192,768]{1,0:T(8,128)(2,1)}, bf16[768,512]{1,0:T(8,128)(2,1)}, bf16[768,512]{1,0:T(8,128)(2,1)}, bf16[512,768]{1,0:T(8,128)(2,1)}) async-done(((bf16[192,2304]{1,0:T(8,128)(2,1)}, bf16[192,768]{1,0:T(8,128)(2,1)}, bf16[768,512]{1,0:T(8,128)(2,1)}, bf16[768,512]{1,0:T(8,128)(2,1)}, bf16[512,768]{1,0:T(8,128)(2,1)}), ...) | async-done | bytes 3538960 | tf_op jit(solution)/shard_map/psum | solution.py:290
  (255 shorter events, 107.5 us)
Async XLA Ops:
  7.2 336.3 %copy-start = (bf16[1,768,2048]{2,1,0:T(8,128)(2,1)S(1)}, bf16[1,768,2048]{2,1,0:T(8,128)(2,1)}, u32[]{:S(2)}) copy-start(bf16[1,768,2048]{2,1,0:T(8,128)(2,1)} %param.24) | copy-start | bytes 9437188
  7.2 63.0 %all-gather.6.cloned.1.call-start = ((), (), s32[]{:S(2)}) async-start(), calls=%async_computation.12 | async-start | bytes 4423680 | tf_op jit(solution)/shard_map/all_gather | solution.py:71
  7.9 103.7 %all-gather.8.cloned.1.call-start = ((), (), s32[]{:S(2)}) async-start(), calls=%async_computation.13 | async-start | bytes 1474560 | tf_op jit(solution)/shard_map/all_gather | solution.py:72
  8.7 126.5 %all-gather.10.cloned.1.call-start = ((), (), s32[]{:S(2)}) async-start(), calls=%async_computation.14 | async-start | bytes 3932160 | tf_op jit(solution)/shard_map/all_gather | solution.py:76
  9.4 171.3 %all-gather.12.cloned.1.call-start = ((), (), s32[]{:S(2)}) async-start(), calls=%async_computation.15 | async-start | bytes 3932160 | tf_op jit(solution)/shard_map/all_gather | solution.py:77
  20.7 8.3 copy-start.18
  45.8 7.3 copy-start.57
  45.8 8.6 %copy-start.60 = (bf16[192]{0:T(256)(128)(2,1)S(1)}, bf16[192]{0:T(256)(128)(2,1)}, u32[]{:S(2)}) copy-start(bf16[192]{0:T(256)(128)(2,1)} %param.17) | copy-start | bytes 1156
  45.8 8.8 %copy-start.61 = (bf16[192]{0:T(256)(128)(2,1)S(1)}, bf16[192]{0:T(256)(128)(2,1)}, u32[]{:S(2)}) copy-start(bf16[192]{0:T(256)(128)(2,1)} %param.20) | copy-start | bytes 1156
  45.8 208.9 %all-to-all-start.2 = ((bf16[8,256,768]{2,1,0:T(8,128)(2,1)}), bf16[8,256,768]{2,1,0:T(8,128)(2,1)}, u32[]{:S(2)}, u32[]{:S(2)}) async-start(bf16[8,256,768]{2,1,0:T(8,128)(2,1)} %bitcast.120), calls=%async_computation.2 | async-start | bytes 6291456 | tf_op jit(solution)/shard_map/all_to_all | solution.py:177
  52.4 174.0 %all-gather.14.cloned.1.call-start = ((), (), s32[]{:S(2)}) async-start(), calls=%async_computation.16 | async-start | bytes 3932160 | tf_op jit(solution)/shard_map/all_gather | solution.py:78
  53.0 643.7 %reduce-scatter.13.cloned.1.call-start = ((), (), s32[]{:S(2)}) async-start(), calls=%async_computation.19 | async-start | bytes 3932160 | tf_op jit(solution)/shard_map/reduce_scatter | solution.py:228
  65.5 9.2 %copy-start.51 = (f32[768]{0:T(1024)}, f32[768]{0:T(1024)S(1)}, u32[]{:S(2)}) copy-start(f32[768]{0:T(1024)S(1)} %convert_element_type.183) | copy-start | bytes 9220
  68.6 36.3 %copy-start.12 = (pred[512,512]{0,1:T(8,128)(4,1)}, pred[512,512]{0,1:T(8,128)(4,1)S(1)}, u32[]{:S(2)}) copy-start(pred[512,512]{0,1:T(8,128)(4,1)S(1)} %fusion.29) | copy-start | bytes 786436
  69.5 14.5 %copy-start.37 = (f32[512,32]{0,1:T(8,128)}, f32[512,32]{0,1:T(8,128)S(1)}, u32[]{:S(2)}) copy-start(f32[512,32]{0,1:T(8,128)S(1)} %get-tuple-element.73) | copy-start | bytes 196612
  70.2 45.1 %copy-start.44 = (f32[768]{0:T(1024)}, f32[768]{0:T(1024)S(1)}, u32[]{:S(2)}) copy-start(f32[768]{0:T(1024)S(1)} %convert_element_type.190) | copy-start | bytes 9220
  86.3 5.8 copy-start.20
  86.3 5.8 copy-start.22
  86.3 5.8 copy-start.25
  86.4 5.8 copy-start.27
  92.2 12.7 %copy-start.40 = (f32[12,512]{1,0:T(8,128)}, f32[12,512]{1,0:T(8,128)S(1)}, u32[]{:S(2)}) copy-start(f32[12,512]{1,0:T(8,128)S(1)} %get-tuple-element.74) | copy-start | bytes 73732
  96.9 8.9 %copy-start.2 = (f32[12,512,512]{1,2,0:T(8,128)S(1)}, f32[12,512,512]{1,2,0:T(8,128)}, u32[]{:S(2)}) copy-start(f32[12,512,512]{1,2,0:T(8,128)} %get-tuple-element.75) | copy-start | bytes 37748740
  226.4 11.3 %copy-start.17 = (bf16[512,768]{1,0:T(8,128)(2,1)S(1)}, bf16[512,768]{1,0:T(8,128)(2,1)}, u32[]{:S(2)}) copy-start(bf16[512,768]{1,0:T(8,128)(2,1)} %multiply_convert_fusion.8) | copy-start | bytes 2359300
  254.7 76.2 %all-to-all-start = ((bf16[8,256,768]{2,1,0:T(8,128)(2,1)}), bf16[8,256,768]{2,1,0:T(8,128)(2,1)}, u32[]{:S(2)}, u32[]{:S(2)}) async-start(bf16[8,256,768]{2,1,0:T(8,128)(2,1)} %bitcast.121), calls=%async_computation | async-start | bytes 6291456 | tf_op jit(solution)/shard_map/all_to_all | solution.py:151
  259.3 437.4 %reduce-scatter.15.cloned.1.call-start = ((), (), s32[]{:S(2)}) async-start(), calls=%async_computation.20 | async-start | bytes 3932160 | tf_op jit(solution)/shard_map/reduce_scatter | solution.py:231
  369.7 10.4 %copy-start.64 = (bf16[2048,2048]{1,0:T(8,128)(2,1)S(1)}, bf16[2048,2048]{1,0:T(8,128)(2,1)}, u32[]{:S(2)}) copy-start(bf16[2048,2048]{1,0:T(8,128)(2,1)} %get-tuple-element.43) | copy-start | bytes 25165828
  388.3 75.1 %all-to-all-start.3 = ((bf16[8,256,768]{2,1,0:T(8,128)(2,1)}), bf16[8,256,768]{2,1,0:T(8,128)(2,1)S(1)}, u32[]{:S(2)}, u32[]{:S(2)}) async-start(bf16[8,256,768]{2,1,0:T(8,128)(2,1)} %bitcast.130), calls=%async_computation.3 | async-start | bytes 6291456 | tf_op jit(solution)/shard_map/all_to_all | solution.py:192
  392.0 304.7 %reduce-scatter.17.cloned.1.call-start = ((), (), s32[]{:S(2)}) async-start(), calls=%async_computation.21 | async-start | bytes 3932160 | tf_op jit(solution)/shard_map/reduce_scatter | solution.py:234
  397.6 299.1 %reduce-scatter.11.cloned.1.call-start = ((), (), s32[]{:S(2)}) async-start(), calls=%async_computation.18 | async-start | bytes 1474560 | tf_op jit(solution)/shard_map/reduce_scatter | solution.py:282
  473.9 5.8 copy-start.47
  486.2 7.0 copy-start.4
  493.2 11.4 %slice-start = ((s8[12582912]{0:T(1024)(128)(4,1)}), s8[4194304]{0:T(1024)(128)(4,1)S(1)}, s32[]{:S(2)}) async-start(s8[12582912]{0:T(1024)(128)(4,1)} %bitcast.114), calls=%async_computation.26 | async-start | bytes 8388608
  493.2 11.4 %slice-start.1 = ((s8[12582912]{0:T(1024)(128)(4,1)}), s8[4194304]{0:T(1024)(128)(4,1)S(1)}, s32[]{:S(2)}) async-start(s8[12582912]{0:T(1024)(128)(4,1)} %bitcast.114), calls=%async_computation.27 | async-start | bytes 8388608
  493.2 12.8 %slice-start.2 = ((s8[12582912]{0:T(1024)(128)(4,1)}), s8[4194304]{0:T(1024)(128)(4,1)S(1)}, s32[]{:S(2)}) async-start(s8[12582912]{0:T(1024)(128)(4,1)} %bitcast.114), calls=%async_computation.28 | async-start | bytes 8388608
  506.0 10.2 %copy-start.26 = (bf16[512,12,32]{0,2,1:T(8,128)(2,1)S(1)}, bf16[512,12,32]{0,2,1:T(8,128)(2,1)}, u32[]{:S(2)}) copy-start(bf16[512,12,32]{0,2,1:T(8,128)(2,1)} %copy-done.25) | copy-start | bytes 1179652
  506.0 10.2 %copy-start.28 = (bf16[512,12,32]{0,2,1:T(8,128)(2,1)S(1)}, bf16[512,12,32]{0,2,1:T(8,128)(2,1)}, u32[]{:S(2)}) copy-start(bf16[512,12,32]{0,2,1:T(8,128)(2,1)} %copy-done.27) | copy-start | bytes 1179652
  516.1 180.6 %reduce-scatter.9.cloned.1.call-start = ((), (), s32[]{:S(2)}) async-start(), calls=%async_computation.17 | async-start | bytes 4423680 | tf_op jit(solution)/shard_map/reduce_scatter | solution.py:279
  516.2 7.5 slice-start.3
  516.2 7.5 slice-start.4
  533.1 183.7 %reduce-scatter.19.cloned.1.call-start = ((), (), s32[]{:S(2)}) async-start(), calls=%async_computation.22 | async-start | bytes 3932160 | tf_op jit(solution)/shard_map/reduce_scatter | solution.py:198
  545.3 174.0 %reduce-scatter.21.cloned.1.call-start = ((), (), s32[]{:S(2)}) async-start(), calls=%async_computation.23 | async-start | bytes 3932160 | tf_op jit(solution)/shard_map/reduce_scatter | solution.py:201
  557.6 176.1 %reduce-scatter.23.cloned.1.call-start = ((), (), s32[]{:S(2)}) async-start(), calls=%async_computation.24 | async-start | bytes 3932160 | tf_op jit(solution)/shard_map/reduce_scatter | solution.py:204
  581.5 75.1 %all-to-all-start.1 = ((bf16[8,256,768]{2,1,0:T(8,128)(2,1)}), bf16[8,256,768]{2,1,0:T(8,128)(2,1)S(1)}, u32[]{:S(2)}, u32[]{:S(2)}) async-start(bf16[8,256,768]{2,1,0:T(8,128)(2,1)} %bitcast.131), calls=%async_computation.1 | async-start | bytes 6291456 | tf_op jit(solution)/shard_map/all_to_all | solution.py:159
  585.1 236.8 %all-reduce.12.cloned.1.call-start = ((), (), s32[]{:S(2)}) async-start(), calls=%async_computation.25 | async-start | bytes 7077888 | tf_op jit(solution)/shard_map/psum | solution.py:290
  672.7 24.1 %copy-start.19 = (f32[512,2]{1,0:T(8,128)S(1)}, f32[512,2]{1,0:T(8,128)}, u32[]{:S(2)}) copy-start(f32[512,2]{1,0:T(8,128)} %copy-done.18) | copy-start | bytes 12292
  696.8 11.4 %copy-start.5 = (f32[512,768]{1,0:T(8,128)S(1)}, f32[512,768]{1,0:T(8,128)}, u32[]{:S(2)}) copy-start(f32[512,768]{1,0:T(8,128)} %copy-done.4) | copy-start | bytes 4718596
  696.8 11.4 %copy-start.53 = (f32[512]{0:T(512)S(1)}, f32[512]{0:T(512)}, u32[]{:S(2)}) copy-start(f32[512]{0:T(512)} %get-tuple-element.65) | copy-start | bytes 6148
  821.9 5.9 copy-start.35
  (41 other events, 136.9 us)
Sparse Core Ops, SparseCore 0:
  9.9 49.9 all-gather.5
  61.7 27.7 all-gather.7
  91.3 43.8 all-gather.9
  136.8 43.8 all-gather.11
  182.4 43.9 all-gather.13
  241.4 43.9 reduce-scatter.12
  288.3 43.9 reduce-scatter.14
  397.7 44.3 reduce-scatter.16
  516.3 26.4 reduce-scatter.10
  545.7 47.2 reduce-scatter.8
  595.9 43.9 reduce-scatter.18
  642.7 44.1 reduce-scatter.20
  689.9 43.7 reduce-scatter.22
  736.3 85.5 all-reduce.11
where the time goes:
time: 845 us; the launch traced here: 837 us
  waiting for transfers between devices  382 us (45%)
  matrix products  222 us (26%)
  local copies, waits for them, and re-layouts  96.1 us (11%)
  other arithmetic  67.4 us (8%)
  blocking collectives  33.4 us (4%)
  starting transfers between devices  19.1 us (2%)
  between operations  17.1 us (2%)
    dot_general x24, matrix products, matmul(): return jnp.dot(left, right, preferred_element_type=jnp.float32)  190 us
    psum x1, waiting for transfers between devices, on_device(): lax.psum(attn_pieces[0].astype(jnp.bfloat16), 'expert').astype(jnp.float32)  85.9 us
    all_to_all x1, waiting for transfers between devices, on_device(): lax.all_to_all(result, 'expert', split_axis=0, concat_axis=0, tiled=True)  70.8 us
    all_to_all x1, waiting for transfers between devices, on_device(): lax.all_to_all(row_grad, 'expert', split_axis=0, concat_axis=0, tiled=True)  59.5 us
    all_to_all x1, waiting for transfers between devices, on_device(): lax.all_to_all(dispatched, 'expert', split_axis=0, concat_axis=0, tiled=T...  53.3 us
    all_gather x1, waiting for transfers between devices, on_device(): lax.all_gather(shared_down, 'shard', axis=0, tiled=True)  39.8 us
    all_gather x1, waiting for transfers between devices, on_device(): lax.all_gather(shared_up, 'shard', axis=1, tiled=True)  39.6 us
    gather x2, local copies, waits for them, and re-layouts, place_rows(): return padded[index].reshape(experts, capacity, model_width)  23 us
  transfers between devices with their start and end apart: 18, of which 8 were waited for; matrix products, arithmetic and copies ran while one was open for 43% of the time, Pallas kernels for 0%

commit v1 on v0

--- a/solution.py
+++ b/solution.py
@@ -66,6 +66,11 @@
     routes,
     prefix,
 ):
+
+    def play_regions(point):
+        main = lax.all_gather(point, "expert").sum(axis=0)
+        return main
+
     length, model_width = inputs.shape
     qkv_full, out_full, gain_one = (
         lax.all_gather(qkv_weight, "shard", axis=0, tiled=True),
@@ -287,7 +292,7 @@
         ).astype(jnp.float32),
     )
     summed = (
-        lax.psum(attn_pieces[0].astype(jnp.bfloat16), "expert").astype(jnp.float32),
+        play_regions(attn_pieces[0].astype(jnp.bfloat16)).astype(jnp.float32),
         lax.psum(attn_pieces[1].astype(jnp.bfloat16), "expert").astype(jnp.float32),
         lax.psum(attn_pieces[2].astype(jnp.bfloat16), "expert").astype(jnp.float32),
         lax.psum(ffn_pieces[0].astype(jnp.bfloat16), "expert").astype(jnp.float32),

time: 845 us -> 901 us (1.066)
  waiting for transfers between devices: 382 us -> 433 us
    all_gather x0 -> x1, waiting for transfers between devices: none -> 65.3 us  [play_regions(): main = lax.all_gather(point, 'expert').sum(axis=0)]
    psum x1, waiting for transfers between devices: 85.9 us -> 59.7 us  [on_device(): lax.psum(attn_pieces[1].astype(jnp.bfloat16), 'expert').astype(jnp.float32)]
    reduce_scatter x1, waiting for transfers between devices: 0.02 us -> 23.1 us  [on_device(): lax.psum_scatter(qkv_weight_grad.astype(jnp.bfloat16), 'shard', scatter_d...]
    reduce_scatter x1, waiting for transfers between devices: 11.9 us -> 0.01 us  [on_device(): lax.psum_scatter(down_term[None].astype(jnp.bfloat16), 'shard', scatter_d...]
  transfers between devices with their start and end apart: 18 -> 19, of which waited for: 8 -> 9; matrix products, arithmetic and copies ran while one was open for 43% -> 41% of each run, Pallas kernels for 0% -> 0%
where the time goes in v1:
time: 901 us; the launch traced here: 894 us
  waiting for transfers between devices  433 us (48%)
  matrix products  222 us (25%)
  local copies, waits for them, and re-layouts  94 us (10%)
  other arithmetic  73.9 us (8%)
  blocking collectives  33.4 us (4%)
  starting transfers between devices  20.4 us (2%)
  between operations  17.1 us (2%)
    dot_general x24, matrix products, matmul(): return jnp.dot(left, right, preferred_element_type=jnp.float32)  190 us
    all_to_all x1, waiting for transfers between devices, on_device(): lax.all_to_all(result, 'expert', split_axis=0, concat_axis=0, tiled=True)  70.8 us
    all_gather x1, waiting for transfers between devices, play_regions(): main = lax.all_gather(point, 'expert').sum(axis=0)  65.3 us
    psum x1, waiting for transfers between devices, on_device(): lax.psum(attn_pieces[1].astype(jnp.bfloat16), 'expert').astype(jnp.float32)  59.7 us
    all_to_all x1, waiting for transfers between devices, on_device(): lax.all_to_all(row_grad, 'expert', split_axis=0, concat_axis=0, tiled=True)  59.5 us
    all_to_all x1, waiting for transfers between devices, on_device(): lax.all_to_all(dispatched, 'expert', split_axis=0, concat_axis=0, tiled=T...  53.1 us
    all_gather x1, waiting for transfers between devices, on_device(): lax.all_gather(shared_down, 'shard', axis=0, tiled=True)  39.8 us
    all_gather x1, waiting for transfers between devices, on_device(): lax.all_gather(shared_up, 'shard', axis=1, tiled=True)  39.6 us
  transfers between devices with their start and end apart: 19, of which 9 were waited for; matrix products, arithmetic and copies ran while one was open for 41% of the time, Pallas kernels for 0%

profile of v1, /device:TPU:0, one launch (start us, length us, event | category | flops | bytes accessed | tf_op | source)
XLA Modules:
  0.0 893.8 jit_solution(8186871518844121848)
XLA Ops:
  15.3 5.3 mul.525
  34.1 11.7 %gather_fusion.2 = bf16[2048,768]{1,0:T(8,128)(2,1)} fusion(bf16[1025,768]{1,0:T(8,128)(2,1)} %concatenate.29, s32[2048]{0:T(1024)S(1)} %get-tuple-element.62), kind=kCustom, calls=%fused_computation.2 | custom fusion | bytes 6299648 | tf_op jit(solution)/shard_map/gather | solution.py:150
  45.9 6.6 all-to-all-start.2
  54.9 10.7 %all-reduce.9 = (bf16[768]{0:T(1024)(128)(2,1)S(1)}, bf16[768]{0:T(1024)(128)(2,1)}) all-reduce(bf16[768]{0:T(1024)(128)(2,1)S(1)} %dynamic-update-slice, bf16[768]{0:T(1024)(128)(2,1)S(1)} %dynamic-update-slice.1), channel_id=1, replica_groups=mesh['expert'=8,'shard'=4] {'shard'}, use_global_device_ids=true, to_apply=%add.2 | all-reduce | flops 1536 | bytes 6144
  86.4 5.8 fusion.7
  96.9 8.0 fusion.1
  105.8 5.9 fusion.28
  117.0 18.2 %all-gather.12.cloned.1.call-done = bf16[768,2048]{1,0:T(8,128)(2,1)} async-done(((bf16[768,512]{1,0:T(8,128)(2,1)}), bf16[768,2048]{1,0:T(8,128)(2,1)}) %all-gather.12.cloned.1.call-update) | async-done | bytes 3145744 | tf_op jit(solution)/shard_map/all_gather | solution.py:81
  135.2 5.9 fusion.62
  141.1 39.6 %all-gather.14.cloned.1.call-done = bf16[768,2048]{1,0:T(8,128)(2,1)} async-done(((bf16[768,512]{1,0:T(8,128)(2,1)}), bf16[768,2048]{1,0:T(8,128)(2,1)}) %all-gather.14.cloned.1.call-update) | async-done | bytes 3145744 | tf_op jit(solution)/shard_map/all_gather | solution.py:82
  180.7 6.0 fusion.63
  186.7 39.8 %all-gather.16.cloned.1.call-done = bf16[2048,768]{1,0:T(8,128)(2,1)} async-done(((bf16[512,768]{1,0:T(8,128)(2,1)}), bf16[2048,768]{1,0:T(8,128)(2,1)}) %all-gather.16.cloned.1.call-update) | async-done | bytes 3145744 | tf_op jit(solution)/shard_map/all_gather | solution.py:83
  226.4 10.0 %multiply_convert_fusion.4 = (bf16[512,2048]{1,0:T(8,128)(2,1)}, bf16[512,2048]{1,0:T(8,128)(2,1)S(1)}, bf16[512,2048]{1,0:T(8,128)(2,1)}) fusion(f32[512,2048]{1,0:T(8,128)} %fusion.62, f32[512,2048]{1,0:T(8,128)} %fusion.63, bf16[2048,768]{1,0:T(8,128)(2,1)} %all-gather.16.cloned.1.call-done, f32[512,768]{1,0:T(8,128)} %param.16), kind=kOutput, calls=%fused_computation.24 | convolution fusion | flops 1626734592 | bytes 19398656 | tf_op jit(solution)/shard_map/dot_general | solution.py:49
  243.3 11.3 %gather_fusion = bf16[2048,768]{1,0:T(8,128)(2,1)} fusion(bf16[513,768]{1,0:T(8,128)(2,1)} %concatenate.28, s32[2048]{0:T(1024)S(1)} %get-tuple-element.63), kind=kCustom, calls=%fused_computation | custom fusion | bytes 6299648 | tf_op jit(solution)/shard_map/gather | solution.py:150
  254.6 4.6 all-to-all-start
  259.3 5.5 convolution_convert_fusion.5
  264.8 12.9 %fusion.9 = f32[2048,2048]{1,0:T(8,128)} fusion(bf16[2048,768]{1,0:T(8,128)(2,1)} %bitcast.18, bf16[1,2048,768]{2,1,0:T(8,128)(2,1)} %param.26), kind=kOutput, calls=%fused_computation.36 | convolution fusion | flops 6442450944 | bytes 23068672 | tf_op jit(solution)/shard_map/dot_general | solution.py:49
  277.8 53.1 %all-to-all-done = bf16[8,256,768]{2,1,0:T(8,128)(2,1)} async-done(((bf16[8,256,768]{2,1,0:T(8,128)(2,1)}), bf16[8,256,768]{2,1,0:T(8,128)(2,1)}, u32[]{:S(2)}, u32[]{:S(2)}) %all-to-all-start) | async-done | bytes 3145760 | tf_op jit(solution)/shard_map/all_to_all | solution.py:156
  330.9 12.7 %fusion.14 = f32[2048,2048]{1,0:T(8,128)} fusion(bf16[2048,768]{1,0:T(8,128)(2,1)} %bitcast.11, bf16[1,768,2048]{2,1,0:T(8,128)(2,1)} %param.25), kind=kOutput, calls=%fused_computation.41 | convolution fusion | flops 6442450944 | bytes 23068672 | tf_op jit(solution)/shard_map/dot_general | solution.py:49
  343.6 26.2 %multiply_convert_fusion.1 = (bf16[2048,2048]{1,0:T(8,128)(2,1)}, bf16[2048,2048]{1,0:T(8,128)(2,1)}, bf16[2048,2048]{1,0:T(8,128)(2,1)}) fusion(f32[2048,2048]{1,0:T(8,128)} %fusion.9, f32[2048,2048]{1,0:T(8,128)} %fusion.14, bf16[2048,768]{1,0:T(8,128)(2,1)} %bitcast.11, bf16[1,768,2048]{2,1,0:T(8,128)(2,1)S(1)} %copy-done), kind=kOutput, calls=%fused_computation.6 | convolution fusion | flops 6505365504 | bytes 65011712 | tf_op jit(solution)/shard_map/dot_general | solution.py:49
  369.8 10.4 %fusion.12 = f32[2048,768]{1,0:T(8,128)S(1)} fusion(bf16[2048,2048]{1,0:T(8,128)(2,1)} %get-tuple-element.43, bf16[1,768,2048]{2,1,0:T(8,128)(2,1)} %param.25), kind=kOutput, calls=%fused_computation.39 | convolution fusion | flops 6442450944 | bytes 17825792 | tf_op jit(solution)/shard_map/dot_general | solution.py:49
  380.2 8.1 add_convert_fusion
  392.1 5.6 convolution_convert_fusion.4
  398.5 5.5 fusion.64
  404.0 59.5 %all-to-all-done.3 = bf16[8,256,768]{2,1,0:T(8,128)(2,1)S(1)} async-done(((bf16[8,256,768]{2,1,0:T(8,128)(2,1)}), bf16[8,256,768]{2,1,0:T(8,128)(2,1)S(1)}, u32[]{:S(2)}, u32[]{:S(2)}) %all-to-all-start.3) | async-done | bytes 3145760 | tf_op jit(solution)/shard_map/all_to_all | solution.py:197
  463.5 5.6 gather_fusion.3
  469.1 4.9 reshape.294
  474.0 5.7 reduce_sum.128
  479.7 5.2 multiply_reduce_fusion.3
  493.3 11.4 %multiply_reduce_fusion = (f32[12,512]{1,0:T(8,128)S(1)}, f32[12,512,512]{1,2,0:T(8,128)}) fusion(f32[12,512]{1,0:T(8,128)S(1)} %log_add_fusion, f32[12,512,512]{1,2,0:T(8,128)} %get-tuple-element.74, pred[512,512]{0,1:T(8,128)(4,1)S(1)} %copy-done.13, bf16[512,12,64]{0,2,1:T(8,128)(2,1)} %bitcast.128, bf16[512,12,64]{0,2,1:T(8,128)(2,1)S(1)} %bitcast.127), kind=kOutput, calls=%fused_computation.11 | convolution fusion | flops 418375680 | bytes 27049984 | tf_op jit(solution)/shard_map/qhd,khd->hqk/dot_general | solution.py:257
  506.1 10.1 %multiply_convert_fusion.3 = bf16[12,512,512]{1,2,0:T(8,128)(2,1)} fusion(f32[12,512,512]{1,2,0:T(8,128)} %get-tuple-element.79, f32[12,512]{1,0:T(8,128)S(1)} %get-tuple-element.78, f32[12,512]{1,0:T(8,128)S(1)} %log_add_fusion, f32[12,512,512]{1,2,0:T(8,128)S(1)} %bitcast.116, pred[512,512]{0,1:T(8,128)(4,1)S(1)} %copy-done.13), kind=kLoop, calls=%fused_computation.10 | loop fusion | flops 18874368 | bytes 31768576 | tf_op jit(solution)/shard_map/convert_element_type | solution.py:262
  533.2 12.2 %fusion.21 = bf16[1,768,2048]{2,1,0:T(8,128)(2,1)} fusion(bf16[2048,768]{1,0:T(8,128)(2,1)} %bitcast.11, bf16[2048,2048]{1,0:T(8,128)(2,1)} %get-tuple-element.42), kind=kOutput, calls=%fused_computation.51 | convolution fusion | flops 6444023808 | bytes 14680064 | tf_op jit(solution)/shard_map/dot_general | solution.py:49
  545.5 12.2 %fusion.22 = bf16[1,768,2048]{2,1,0:T(8,128)(2,1)} fusion(bf16[2048,768]{1,0:T(8,128)(2,1)} %bitcast.11, bf16[2048,2048]{1,0:T(8,128)(2,1)} %get-tuple-element.43), kind=kOutput, calls=%fused_computation.52 | convolution fusion | flops 6444023808 | bytes 14680064 | tf_op jit(solution)/shard_map/dot_general | solution.py:49
  557.7 11.6 %fusion.20 = bf16[1,2048,768]{2,1,0:T(8,128)(2,1)} fusion(bf16[2048,2048]{1,0:T(8,128)(2,1)} %get-tuple-element.44, bf16[2048,768]{1,0:T(8,128)(2,1)} %bitcast.18), kind=kOutput, calls=%fused_computation.50 | convolution fusion | flops 6444023808 | bytes 14680064 | tf_op jit(solution)/shard_map/dot_general | solution.py:49
  570.0 23.1 %reduce-scatter.9.cloned.1.call-done = bf16[192,2304]{1,0:T(8,128)(2,1)} async-done(((bf16[768,2304]{1,0:T(8,128)(2,1)}), bf16[192,2304]{1,0:T(8,128)(2,1)}) %reduce-scatter.9.cloned.1.call-update) | async-done | bytes 884752 | tf_op jit(solution)/shard_map/reduce_scatter | solution.py:284
  593.1 10.2 %convolution_convert_fusion.3 = bf16[2048,768]{1,0:T(8,128)(2,1)} fusion(bf16[2048,2048]{1,0:T(8,128)(2,1)} %get-tuple-element.44, bf16[1,2048,768]{2,1,0:T(8,128)(2,1)S(1)} %copy-done.57), kind=kOutput, calls=%fused_computation.31 | convolution fusion | flops 6444023808 | bytes 14680064 | tf_op jit(solution)/shard_map/dot_general | solution.py:49
  603.2 4.9 all-to-all-start.1
  608.8 70.8 %all-to-all-done.1 = bf16[8,256,768]{2,1,0:T(8,128)(2,1)S(1)} async-done(((bf16[8,256,768]{2,1,0:T(8,128)(2,1)}), bf16[8,256,768]{2,1,0:T(8,128)(2,1)S(1)}, u32[]{:S(2)}, u32[]{:S(2)}) %all-to-all-start.1) | async-done | bytes 3145760 | tf_op jit(solution)/shard_map/all_to_all | solution.py:164
  679.6 5.2 gather_fusion.1
  684.8 5.0 reshape.293
  689.9 5.6 multiply_reduce_fusion.4
  695.5 9.1 %all-reduce.8 = (bf16[768]{0:T(1024)(128)(2,1)S(1)}, bf16[768]{0:T(1024)(128)(2,1)S(1)}) all-reduce(bf16[768]{0:T(1024)(128)(2,1)S(1)} %get-tuple-element.30, bf16[768]{0:T(1024)(128)(2,1)S(1)} %get-tuple-element.28), channel_id=3, replica_groups=mesh['expert'=8,'shard'=4] {'shard'}, use_global_device_ids=true, to_apply=%region_14.15.clone | all-reduce | flops 1536 | bytes 6144
  704.8 13.6 %all-reduce.6 = (bf16[192]{0:T(256)(128)(2,1)S(1)}, bf16[192]{0:T(256)(128)(2,1)S(1)}) all-reduce(bf16[192]{0:T(256)(128)(2,1)S(1)} %dynamic-slice.3, bf16[192]{0:T(256)(128)(2,1)S(1)} %dynamic-slice.5), channel_id=1, replica_groups=mesh['expert'=8,'shard'=4] {'expert'}, use_global_device_ids=true, to_apply=%region_15.16 | all-reduce | flops 384 | bytes 1536 | tf_op jit(solution)/shard_map/psum | solution.py:297
  719.5 9.7 %multiply_reduce_fusion.1 = (f32[512,2]{1,0:T(8,128)}, f32[512,768]{1,0:T(8,128)}) fusion(f32[512,2,768]{2,1,0:T(2,128)} %reshape.293, f32[512,768]{1,0:T(8,128)} %param.16, f32[512,2]{1,0:T(8,128)S(1)} %copy-done.19), kind=kLoop, calls=%fused_computation.47 | loop fusion | flops 2751488 | bytes 6299648 | tf_op jit(solution)/shard_map/reduce_sum | solution.py:175
  734.9 4.6 add_add_fusion.1
  746.9 59.7 %all-reduce.12.cloned.1.call-done = (bf16[192,768]{1,0:T(8,128)(2,1)}, bf16[768,512]{1,0:T(8,128)(2,1)}, bf16[768,512]{1,0:T(8,128)(2,1)}, bf16[512,768]{1,0:T(8,128)(2,1)}) async-done(((bf16[192,768]{1,0:T(8,128)(2,1)}, bf16[768,512]{1,0:T(8,128)(2,1)}, bf16[768,512]{1,0:T(8,128)(2,1)}, bf16[512,768]{1,0:T(8,128)(2,1)}), (bf16[192,768]{1,0:T(8,128)(2,1)}, bf16[768,512]{1,0:T(8,128)(2,1)}, ...) | async-done | bytes 2654224 | tf_op jit(solution)/shard_map/psum | solution.py:296
  813.7 65.3 %all-gather.18.cloned.1.call-done = bf16[1536,2304]{1,0:T(8,128)(2,1)} async-done(((bf16[192,2304]{1,0:T(8,128)(2,1)}), bf16[1536,2304]{1,0:T(8,128)(2,1)}) %all-gather.18.cloned.1.call-update) | async-done | bytes 7077904 | tf_op jit(solution)/shard_map/all_gather | solution.py:71
  878.9 5.4 reduce_sum.133
  (257 shorter events, 116.6 us)
Async XLA Ops:
  7.2 336.4 %copy-start = (bf16[1,768,2048]{2,1,0:T(8,128)(2,1)S(1)}, bf16[1,768,2048]{2,1,0:T(8,128)(2,1)}, u32[]{:S(2)}) copy-start(bf16[1,768,2048]{2,1,0:T(8,128)(2,1)} %param.24) | copy-start | bytes 9437188
  7.2 63.1 %all-gather.8.cloned.1.call-start = ((), (), s32[]{:S(2)}) async-start(), calls=%async_computation.12 | async-start | bytes 4423680 | tf_op jit(solution)/shard_map/all_gather | solution.py:76
  7.9 103.8 %all-gather.10.cloned.1.call-start = ((), (), s32[]{:S(2)}) async-start(), calls=%async_computation.13 | async-start | bytes 1474560 | tf_op jit(solution)/shard_map/all_gather | solution.py:77
  8.7 126.5 %all-gather.12.cloned.1.call-start = ((), (), s32[]{:S(2)}) async-start(), calls=%async_computation.14 | async-start | bytes 3932160 | tf_op jit(solution)/shard_map/all_gather | solution.py:81
  9.4 171.3 %all-gather.14.cloned.1.call-start = ((), (), s32[]{:S(2)}) async-start(), calls=%async_computation.15 | async-start | bytes 3932160 | tf_op jit(solution)/shard_map/all_gather | solution.py:82
  20.7 8.3 copy-start.18
  45.8 7.3 copy-start.56
  45.9 8.6 copy-start.59
  45.9 8.8 copy-start.60
  45.9 208.8 %all-to-all-start.2 = ((bf16[8,256,768]{2,1,0:T(8,128)(2,1)}), bf16[8,256,768]{2,1,0:T(8,128)(2,1)}, u32[]{:S(2)}, u32[]{:S(2)}) async-start(bf16[8,256,768]{2,1,0:T(8,128)(2,1)} %bitcast.121), calls=%async_computation.2 | async-start | bytes 6291456 | tf_op jit(solution)/shard_map/all_to_all | solution.py:182
  52.5 173.9 %all-gather.16.cloned.1.call-start = ((), (), s32[]{:S(2)}) async-start(), calls=%async_computation.16 | async-start | bytes 3932160 | tf_op jit(solution)/shard_map/all_gather | solution.py:83
  53.1 516.3 %reduce-scatter.13.cloned.1.call-start = ((), (), s32[]{:S(2)}) async-start(), calls=%async_computation.19 | async-start | bytes 3932160 | tf_op jit(solution)/shard_map/reduce_scatter | solution.py:233
  65.6 9.2 %copy-start.50 = (f32[768]{0:T(1024)}, f32[768]{0:T(1024)S(1)}, u32[]{:S(2)}) copy-start(f32[768]{0:T(1024)S(1)} %convert_element_type.185) | copy-start | bytes 9220
  68.6 36.3 %copy-start.12 = (pred[512,512]{0,1:T(8,128)(4,1)}, pred[512,512]{0,1:T(8,128)(4,1)S(1)}, u32[]{:S(2)}) copy-start(pred[512,512]{0,1:T(8,128)(4,1)S(1)} %fusion.29) | copy-start | bytes 786436
  69.6 14.5 %copy-start.36 = (f32[512,32]{0,1:T(8,128)}, f32[512,32]{0,1:T(8,128)S(1)}, u32[]{:S(2)}) copy-start(f32[512,32]{0,1:T(8,128)S(1)} %get-tuple-element.72) | copy-start | bytes 196612
  70.2 45.1 %copy-start.43 = (f32[768]{0:T(1024)}, f32[768]{0:T(1024)S(1)}, u32[]{:S(2)}) copy-start(f32[768]{0:T(1024)S(1)} %convert_element_type.192) | copy-start | bytes 9220
  86.4 5.8 copy-start.20
  86.4 5.8 copy-start.22
  86.4 5.8 copy-start.25
  92.2 12.7 %copy-start.39 = (f32[12,512]{1,0:T(8,128)}, f32[12,512]{1,0:T(8,128)S(1)}, u32[]{:S(2)}) copy-start(f32[12,512]{1,0:T(8,128)S(1)} %get-tuple-element.73) | copy-start | bytes 73732
  96.9 8.9 copy-start.2
  226.4 11.3 %copy-start.17 = (bf16[512,768]{1,0:T(8,128)(2,1)S(1)}, bf16[512,768]{1,0:T(8,128)(2,1)}, u32[]{:S(2)}) copy-start(bf16[512,768]{1,0:T(8,128)(2,1)} %multiply_convert_fusion.8) | copy-start | bytes 2359300
  254.6 76.2 %all-to-all-start = ((bf16[8,256,768]{2,1,0:T(8,128)(2,1)}), bf16[8,256,768]{2,1,0:T(8,128)(2,1)}, u32[]{:S(2)}, u32[]{:S(2)}) async-start(bf16[8,256,768]{2,1,0:T(8,128)(2,1)} %bitcast.122), calls=%async_computation | async-start | bytes 6291456 | tf_op jit(solution)/shard_map/all_to_all | solution.py:156
  259.2 310.2 %reduce-scatter.15.cloned.1.call-start = ((), (), s32[]{:S(2)}) async-start(), calls=%async_computation.20 | async-start | bytes 3932160 | tf_op jit(solution)/shard_map/reduce_scatter | solution.py:236
  369.8 10.4 %copy-start.63 = (bf16[2048,2048]{1,0:T(8,128)(2,1)S(1)}, bf16[2048,2048]{1,0:T(8,128)(2,1)}, u32[]{:S(2)}) copy-start(bf16[2048,2048]{1,0:T(8,128)(2,1)} %get-tuple-element.42) | copy-start | bytes 25165828
  388.4 75.1 %all-to-all-start.3 = ((bf16[8,256,768]{2,1,0:T(8,128)(2,1)}), bf16[8,256,768]{2,1,0:T(8,128)(2,1)S(1)}, u32[]{:S(2)}, u32[]{:S(2)}) async-start(bf16[8,256,768]{2,1,0:T(8,128)(2,1)} %bitcast.132), calls=%async_computation.3 | async-start | bytes 6291456 | tf_op jit(solution)/shard_map/all_to_all | solution.py:197
  392.0 177.4 %reduce-scatter.17.cloned.1.call-start = ((), (), s32[]{:S(2)}) async-start(), calls=%async_computation.21 | async-start | bytes 3932160 | tf_op jit(solution)/shard_map/reduce_scatter | solution.py:239
  397.7 171.8 %reduce-scatter.11.cloned.1.call-start = ((), (), s32[]{:S(2)}) async-start(), calls=%async_computation.18 | async-start | bytes 1474560 | tf_op jit(solution)/shard_map/reduce_scatter | solution.py:287
  486.2 7.0 copy-start.4
  493.3 11.4 %slice-start = ((s8[12582912]{0:T(1024)(128)(4,1)}), s8[4194304]{0:T(1024)(128)(4,1)S(1)}, s32[]{:S(2)}) async-start(s8[12582912]{0:T(1024)(128)(4,1)} %bitcast.115), calls=%async_computation.27 | async-start | bytes 8388608
  493.3 11.4 %slice-start.1 = ((s8[12582912]{0:T(1024)(128)(4,1)}), s8[4194304]{0:T(1024)(128)(4,1)S(1)}, s32[]{:S(2)}) async-start(s8[12582912]{0:T(1024)(128)(4,1)} %bitcast.115), calls=%async_computation.28 | async-start | bytes 8388608
  493.3 12.8 %slice-start.2 = ((s8[12582912]{0:T(1024)(128)(4,1)}), s8[4194304]{0:T(1024)(128)(4,1)S(1)}, s32[]{:S(2)}) async-start(s8[12582912]{0:T(1024)(128)(4,1)} %bitcast.115), calls=%async_computation.29 | async-start | bytes 8388608
  506.1 10.2 %copy-start.26 = (bf16[512,12,32]{0,2,1:T(8,128)(2,1)S(1)}, bf16[512,12,32]{0,2,1:T(8,128)(2,1)}, u32[]{:S(2)}) copy-start(bf16[512,12,32]{0,2,1:T(8,128)(2,1)} %copy-done.25) | copy-start | bytes 1179652
  506.1 10.2 %copy-start.28 = (bf16[512,12,32]{0,2,1:T(8,128)(2,1)S(1)}, bf16[512,12,32]{0,2,1:T(8,128)(2,1)}, u32[]{:S(2)}) copy-start(bf16[512,12,32]{0,2,1:T(8,128)(2,1)} %copy-done.27) | copy-start | bytes 1179652
  516.2 76.8 %reduce-scatter.9.cloned.1.call-start = ((), (), s32[]{:S(2)}) async-start(), calls=%async_computation.17 | async-start | bytes 4423680 | tf_op jit(solution)/shard_map/reduce_scatter | solution.py:284
  516.3 7.5 slice-start.3
  516.3 7.5 slice-start.4
  533.1 206.4 %reduce-scatter.19.cloned.1.call-start = ((), (), s32[]{:S(2)}) async-start(), calls=%async_computation.22 | async-start | bytes 3932160 | tf_op jit(solution)/shard_map/reduce_scatter | solution.py:203
  545.4 196.6 %reduce-scatter.21.cloned.1.call-start = ((), (), s32[]{:S(2)}) async-start(), calls=%async_computation.23 | async-start | bytes 3932160 | tf_op jit(solution)/shard_map/reduce_scatter | solution.py:206
  557.7 186.8 %reduce-scatter.23.cloned.1.call-start = ((), (), s32[]{:S(2)}) async-start(), calls=%async_computation.24 | async-start | bytes 3932160 | tf_op jit(solution)/shard_map/reduce_scatter | solution.py:209
  569.3 23.7 %copy-start.57 = (bf16[1,2048,768]{2,1,0:T(8,128)(2,1)S(1)}, bf16[1,2048,768]{2,1,0:T(8,128)(2,1)}, u32[]{:S(2)}) copy-start(bf16[1,2048,768]{2,1,0:T(8,128)(2,1)} %param.26) | copy-start | bytes 9437188
  569.3 237.3 %all-reduce.12.cloned.1.call-start = ((), (), s32[]{:S(2)}) async-start(), calls=%async_computation.26 | async-start | bytes 5308416 | tf_op jit(solution)/shard_map/psum | solution.py:296
  569.9 309.0 %all-gather.18.cloned.1.call-start = ((), (), s32[]{:S(2)}) async-start(), calls=%async_computation.25 | async-start | bytes 7962624 | tf_op jit(solution)/shard_map/all_gather | solution.py:71
  603.2 76.4 %all-to-all-start.1 = ((bf16[8,256,768]{2,1,0:T(8,128)(2,1)}), bf16[8,256,768]{2,1,0:T(8,128)(2,1)S(1)}, u32[]{:S(2)}, u32[]{:S(2)}) async-start(bf16[8,256,768]{2,1,0:T(8,128)(2,1)} %bitcast.133), calls=%async_computation.1 | async-start | bytes 6291456 | tf_op jit(solution)/shard_map/all_to_all | solution.py:164
  689.9 29.6 %copy-start.19 = (f32[512,2]{1,0:T(8,128)S(1)}, f32[512,2]{1,0:T(8,128)}, u32[]{:S(2)}) copy-start(f32[512,2]{1,0:T(8,128)} %copy-done.18) | copy-start | bytes 12292
  719.5 11.4 %copy-start.5 = (f32[512,768]{1,0:T(8,128)S(1)}, f32[512,768]{1,0:T(8,128)}, u32[]{:S(2)}) copy-start(f32[512,768]{1,0:T(8,128)} %copy-done.4) | copy-start | bytes 4718596
  719.5 11.4 %copy-start.52 = (f32[512]{0:T(512)S(1)}, f32[512]{0:T(512)}, u32[]{:S(2)}) copy-start(f32[512]{0:T(512)} %get-tuple-element.64) | copy-start | bytes 6148
  878.9 7.9 copy-start.1
  (41 other events, 143.7 us)
Sparse Core Ops, SparseCore 0:
  9.9 49.9 all-gather.7
  61.7 27.7 all-gather.9
  91.3 43.8 all-gather.11
  136.8 43.8 all-gather.13
  182.4 43.9 all-gather.15
  241.4 43.9 reduce-scatter.12
  288.3 43.9 reduce-scatter.14
  397.8 44.3 reduce-scatter.16
  516.3 26.4 reduce-scatter.10
  545.8 47.2 reduce-scatter.8
  596.0 43.9 reduce-scatter.18
  642.8 43.9 reduce-scatter.20
  689.8 44.0 reduce-scatter.22
  736.4 70.2 all-reduce.11
  808.1 70.7 all-gather.17
